TPU v7x, 32 devices: a whole 2x2x4 slice. The times are simulated.
32 devices in a mesh: frame: 8 (over y, x, core), module: 4 (over z).
Axes of the slice: x: 2, y: 2, z: 4, core: 2. Of those that a mesh axis runs over, the one named last changes fastest.
Arguments:
- raw_frames: int32 [2048, 32768], P('frame', 'module'), may hold values from 256 to 3856
- dark_frame: float32 [32768], P('module'), may hold values from 0 to 240
- flat_field: float32 [32768], P('module'), may hold values from 0.125 to 2.625, as said below
- membership: int32 [16, 32768], P(None, 'module'), may hold values from 0 to 1, as said below
Outputs:
- correlation: float32 [16, 8, 5, 256, 256], P('module', 'frame')
Inputs may be any that keep to these rules, and one draw needn't show every extreme that they name: `membership`: each pixel belongs to exactly one q-bin, and every module holds exactly 512 pixels of each q-bin, in no particular order. `flat_field`: positive gains.
All inputs are finite; a program needn't handle non-finite values.
Results may differ from a plain program's by a relative error of at most 0.0003.
Values may be sent and summed in bfloat16 or wider, within the bound.
A program may use at most 128 MiB of HBM per device.

v0:
```python
import jax
import jax.numpy as jnp
from jax import lax
from jax.sharding import PartitionSpec as P


def shifted(value, axis, steps):
    count = lax.axis_size(axis)
    leading, last = (max(0, -steps), min(count, count - steps))
    return lax.ppermute(value, axis, [(source, source + steps) for source in range(leading, last)])


def bin_grams(target, partners):
    return jnp.stack(
        [
            jnp.einsum("urp,vrp->ruv", target, partner, preferred_element_type=jnp.float32)
            for partner in partners
        ],
        axis=1,
    )


def per_device(raw_frames, dark_frame, flat_field, membership):
    block_len = raw_frames.shape[0]
    bin_total, pixel_count = membership.shape
    per_bin = pixel_count // bin_total
    modules = lax.axis_size("module")
    labels = jnp.sum(membership * jnp.arange(bin_total, dtype=jnp.int32)[:, None], axis=0)
    ordering = jnp.argsort(labels, stable=True)
    grouped_raw = jnp.take(raw_frames, ordering, axis=1)
    dark_sorted = jnp.take(dark_frame, ordering)
    flat_sorted = jnp.take(flat_field, ordering)
    intensity = (grouped_raw.astype(jnp.float32) - dark_sorted[None, :]) * flat_sorted[None, :]
    intensity = intensity.reshape(block_len, bin_total, per_bin)
    local_sums = jnp.sum(intensity, axis=2)
    bin_sums = lax.psum(local_sums, "module")
    weight = jnp.sqrt(jnp.float32(per_bin * modules))
    scaled = (intensity * (weight / bin_sums)[:, :, None]).astype(jnp.bfloat16)
    next_one = shifted(scaled, "frame", -1)
    next_two = shifted(scaled, "frame", -2)
    partners = [scaled, next_one, next_two]
    gram_blocks = lax.psum_scatter(
        bin_grams(scaled, [member for member in partners]),
        "module",
        scatter_dimension=0,
        tiled=True,
    )
    back_one = shifted(gram_blocks[:, 1], "frame", 1)
    back_two = shifted(gram_blocks[:, 2], "frame", 2)
    earlier = jnp.swapaxes(jnp.stack([back_two, back_one], axis=1), 2, 3)
    return jnp.concatenate([earlier, gram_blocks], axis=1)[:, None]


def solution(mesh):
    in_specs = (P("frame", "module"), P("module"), P("module"), P(None, "module"))
    out_specs = P("module", "frame", None, None, None)
    return jax.shard_map(
        per_device, mesh=mesh, in_specs=in_specs, out_specs=out_specs, check_vma=False
    )
```

profile of v0, /device:TPU:12, one launch (start us, length us, event | category | flops | bytes accessed | tf_op | source)
XLA Modules:
  0.0 814.2 jit_solution(10648786206379636123)
XLA Ops:
  7.7 6.8 sort.17
  14.5 45.5 %gather_fusion.1 = f32[8192]{0:T(1024)S(1)} fusion(f32[8192]{0:T(1024)S(1)} %copy-done, s32[8192]{0:T(1024)S(1)} %fusion.1), kind=kCustom, calls=%fused_computation.clone | custom fusion | bytes 98304 | tf_op jit(solution)/shard_map/jit(_take)/gather | solution.py:31
  60.8 45.5 %gather_fusion.2 = f32[8192]{0:T(1024)S(1)} fusion(f32[8192]{0:T(1024)S(1)} %copy-done.2, s32[8192]{0:T(1024)S(1)} %fusion.1), kind=kCustom, calls=%fused_computation.1.clone | custom fusion | bytes 98304 | tf_op jit(solution)/shard_map/jit(_take)/gather | solution.py:32
  106.4 9.0 %copy.14 = s32[256,8192]{0,1:T(8,128)} copy(s32[256,8192]{1,0:T(8,128)} %param.6) | data formatting | bytes 16777216 | tf_op args[0]
  115.4 34.7 %gather_fusion = s32[8192,256]{1,0:T(8,128)} fusion(s32[256,8192]{0,1:T(8,128)} %copy.14, s32[8192]{0:T(1024)S(1)} %fusion.1), kind=kCustom, calls=%fused_computation.2 | custom fusion | bytes 16809984 | tf_op jit(solution)/shard_map/jit(_take)/gather | solution.py:30
  150.2 9.3 %copy.15 = s32[256,16,512]{2,0,1:T(8,128)} copy(s32[256,16,512]{0,2,1:T(8,128)} %bitcast.30) | data formatting | bytes 16777216 | tf_op jit(solution)/shard_map/jit(_take)/gather | solution.py:30
  159.4 4.8 fusion
  164.3 15.4 %psum.7 = f32[256,16]{0,1:T(8,128)S(1)} all-reduce(f32[256,16]{0,1:T(8,128)S(1)} %fusion), channel_id=1, replica_groups=mesh['frame'=8,'module'=4] {'module'}, use_global_device_ids=true, to_apply=%region_3.5 | all-reduce | flops 4096 | bytes 32768 | tf_op jit(solution)/shard_map/psum | solution.py:36
  179.7 4.5 multiply_convert_fusion
  184.2 1.9 collective-permute-start
  186.1 3.5 collective-permute-start.1
  190.9 83.2 %collective-permute-done = bf16[256,16,512]{2,0,1:T(8,128)(2,1)S(1)} collective-permute-done((bf16[256,16,512]{2,0,1:T(8,128)(2,1)S(1)}, bf16[256,16,512]{2,0,1:T(8,128)(2,1)S(1)}, u32[]{:S(2)}, u32[]{:S(2)}) %collective-permute-start) | collective-permute-done | bytes 4194336 | tf_op jit(solution)/shard_map/ppermute | solution.py:10
  274.2 3.2 convolution_bitcast_fusion.1
  277.4 46.6 %collective-permute-done.1 = bf16[256,16,512]{2,0,1:T(8,128)(2,1)S(1)} collective-permute-done((bf16[256,16,512]{2,0,1:T(8,128)(2,1)S(1)}, bf16[256,16,512]{2,0,1:T(8,128)(2,1)S(1)}, u32[]{:S(2)}, u32[]{:S(2)}) %collective-permute-start.1) | collective-permute-done | bytes 4194336 | tf_op jit(solution)/shard_map/ppermute | solution.py:10
  323.9 3.3 convolution_bitcast_fusion
  327.2 9.4 %pad_maximum_fusion = f32[16,3,256,256]{3,2,0,1:T(8,128)} fusion(f32[16,1,256,256]{3,2,0,1:T(8,128)} %convolution_bitcast_fusion, f32[16,1,256,256]{3,2,0,1:T(8,128)} %convolution_bitcast_fusion.1, f32[16,1,256,256]{3,2,0,1:T(8,128)S(1)} %convolution_bitcast_fusion.2), kind=kLoop, calls=%fused_computation.3 | loop fusion | flops 6291456 | bytes 25165824 | tf_op jit(solution)/shard_map/stack | solution.py:14
  338.5 423.1 %all-reduce.3.cloned.1.call-done = f32[16,3,256,256]{3,2,0,1:T(8,128)} async-done(((f32[16,3,256,256]{3,2,0,1:T(8,128)}), f32[16,3,256,256]{3,2,0,1:T(8,128)}) %all-reduce.3.cloned.1.call-update) | async-done | bytes 12582928
  761.6 1.8 constant_dynamic-slice_fusion.1
  763.7 3.4 collective-permute-start.2
  767.4 1.9 collective-permute-start.3
  769.4 2.3 constant_dynamic-slice_fusion.2
  771.6 21.0 %collective-permute-done.2 = f32[4,256,256]{1,2,0:T(8,128)} collective-permute-done((f32[4,256,256]{1,2,0:T(8,128)S(1)}, f32[4,256,256]{1,2,0:T(8,128)}, u32[]{:S(2)}, u32[]{:S(2)}) %collective-permute-start.2) | collective-permute-done | bytes 1048608 | tf_op jit(solution)/shard_map/ppermute | solution.py:10
  792.6 9.8 %collective-permute-done.3 = f32[4,256,256]{1,2,0:T(8,128)S(1)} collective-permute-done((f32[4,256,256]{1,2,0:T(8,128)S(1)}, f32[4,256,256]{1,2,0:T(8,128)S(1)}, u32[]{:S(2)}, u32[]{:S(2)}) %collective-permute-start.3) | collective-permute-done | bytes 1048608 | tf_op jit(solution)/shard_map/ppermute | solution.py:10
  804.4 2.9 copy.18
  (25 shorter events, 7.0 us)
Async XLA Ops:
  6.5 8.0 copy-start
  6.5 755.1 %all-reduce.3.cloned.1.call-start = ((), (), s32[]{:S(2)}) async-start(), calls=%async_computation | async-start | bytes 25165824
  60.0 0.8 copy-start.2
  184.2 90.0 %collective-permute-start = (bf16[256,16,512]{2,0,1:T(8,128)(2,1)S(1)}, bf16[256,16,512]{2,0,1:T(8,128)(2,1)S(1)}, u32[]{:S(2)}, u32[]{:S(2)}) collective-permute-start(bf16[256,16,512]{2,0,1:T(8,128)(2,1)S(1)} %multiply_convert_fusion), channel_id=1, source_target_pairs={{4,0},{8,4},{12,8},{16,12},{20,16},{24,20},{28,24},{5,1},{9,5},{13... | collective-permute-start | bytes 12582920 | tf_op jit(solution)/shard_map/ppermute | solution.py:10
  186.1 137.8 %collective-permute-start.1 = (bf16[256,16,512]{2,0,1:T(8,128)(2,1)S(1)}, bf16[256,16,512]{2,0,1:T(8,128)(2,1)S(1)}, u32[]{:S(2)}, u32[]{:S(2)}) collective-permute-start(bf16[256,16,512]{2,0,1:T(8,128)(2,1)S(1)} %multiply_convert_fusion), channel_id=1, source_target_pairs={{8,0},{12,4},{16,8},{20,12},{24,16},{28,20},{9,1},{13,5},{17,9},{2... | collective-permute-start | bytes 12582920 | tf_op jit(solution)/shard_map/ppermute | solution.py:10
  336.6 0.7 copy-start.3
  763.7 28.9 %collective-permute-start.2 = (f32[4,256,256]{1,2,0:T(8,128)S(1)}, f32[4,256,256]{1,2,0:T(8,128)}, u32[]{:S(2)}, u32[]{:S(2)}) collective-permute-start(f32[4,256,256]{1,2,0:T(8,128)S(1)} %bitcast.31), channel_id=1, source_target_pairs={{0,8},{4,12},{8,16},{12,20},{16,24},{20,28},{1,9},{5,13},{9,17},{1... | collective-permute-start | bytes 3145736 | tf_op jit(solution)/shard_map/ppermute | solution.py:10
  767.4 35.0 %collective-permute-start.3 = (f32[4,256,256]{1,2,0:T(8,128)S(1)}, f32[4,256,256]{1,2,0:T(8,128)S(1)}, u32[]{:S(2)}, u32[]{:S(2)}) collective-permute-start(f32[4,256,256]{1,2,0:T(8,128)S(1)} %bitcast.32), channel_id=1, source_target_pairs={{0,4},{4,8},{8,12},{12,16},{16,20},{20,24},{24,28},{1,5},{5,9},{9,... | collective-permute-start | bytes 3145736 | tf_op jit(solution)/shard_map/ppermute | solution.py:10
  803.9 3.4 copy-start.1
Sparse Core Ops, SparseCore 0:
  336.7 424.8 all-reduce.2
where the time goes:
time: 817 us; the launch traced here: 814 us
  waiting for transfers between devices  584 us (71%)
  local copies, waits for them, and re-layouts  154 us (19%)
  other arithmetic  28.5 us (3%)
  blocking collectives  15.4 us (2%)
  between operations  14.2 us (2%)
  starting transfers between devices  10.7 us (1%)
    unnamed x2, waiting for transfers between devices  423 us
    ppermute x4, waiting for transfers between devices, shifted(): lax.ppermute(value, axis, [(source, source + steps) for source in range(l...  161 us
    gather x1, local copies, waits for them, and re-layouts, per_device(): dark_sorted = jnp.take(dark_frame, ordering)  45.5 us
    gather x1, local copies, waits for them, and re-layouts, per_device(): flat_sorted = jnp.take(flat_field, ordering)  45.5 us
    gather x2, local copies, waits for them, and re-layouts, per_device(): grouped_raw = jnp.take(raw_frames, ordering, axis=1)  44 us
  transfers between devices with their start and end apart: 5, of which 5 were waited for; matrix products, arithmetic and copies ran while one was open for 1% of the time, Pallas kernels for 0%

commit v1 on v0

v1 whole, which is shorter than its diff:
```python
import functools

import jax
import jax.numpy as jnp
from jax import lax
from jax.experimental import pallas as pl
from jax.experimental.pallas import tpu as pltpu
from jax.sharding import PartitionSpec as P

MESH = pl.DeviceIdType.MESH
VMEM_BYTES = 60 * 1024 * 1024


def group_kernel(per_bin, order, raw, dark, flat, grouped, sums, turned):
    step = pl.program_id(0)
    chunk = raw.shape[1]
    intensity = (raw[...].astype(jnp.float32) - dark[...]) * flat[...]
    turned[pl.ds(pl.multiple_of(step * chunk, chunk), chunk), :] = intensity.T

    @pl.when(step == pl.num_programs(0) - 1)
    def _():
        frames = turned.shape[1]
        lane = lax.broadcasted_iota(jnp.int32, (8, frames), 0)

        @pl.loop(0, grouped.shape[0])
        def _(label):
            base = label * per_bin

            def rows(group, total):
                first = pl.multiple_of(group * 8, 8)
                tile = jnp.broadcast_to(turned[pl.ds(order[base + first], 1), :], (8, frames))
                for row in range(1, 8):
                    line = turned[pl.ds(order[base + first + row], 1), :]
                    tile = jnp.where(lane == row, line, tile)
                grouped[label, pl.ds(first, 8), :] = tile
                return total + tile

            total = lax.fori_loop(0, per_bin // 8, rows, jnp.zeros((8, frames), jnp.float32), unroll=4)
            sums[pl.ds(label, 1), :] = jnp.sum(total, axis=0, keepdims=True)


def group_by_bin(order, raw_frames, dark_frame, flat_field, bins):
    frames, pixels = raw_frames.shape
    per_bin = pixels // bins
    chunk = per_bin
    return pl.pallas_call(
        functools.partial(group_kernel, per_bin),
        out_shape=(
            jax.ShapeDtypeStruct((bins, per_bin, frames), jnp.float32),
            jax.ShapeDtypeStruct((bins, frames), jnp.float32),
        ),
        grid_spec=pltpu.PrefetchScalarGridSpec(
            num_scalar_prefetch=1,
            grid=(pixels // chunk,),
            in_specs=[
                pl.BlockSpec((frames, chunk), lambda i, o: (0, i)),
                pl.BlockSpec((1, chunk), lambda i, o: (0, i)),
                pl.BlockSpec((1, chunk), lambda i, o: (0, i)),
            ],
            out_specs=(
                pl.BlockSpec((bins, per_bin, frames), lambda i, o: (0, 0, 0)),
                pl.BlockSpec((bins, frames), lambda i, o: (0, 0)),
            ),
            scratch_shapes=[pltpu.VMEM((pixels, frames), jnp.float32)],
        ),
        compiler_params=pltpu.CompilerParams(vmem_limit_bytes=VMEM_BYTES),
    )(order, raw_frames, dark_frame[None, :], flat_field[None, :])


def gram(left, right):
    return lax.dot_general(
        left, right, (((0,), (0,)), ((), ())), preferred_element_type=jnp.float32
    )


def correlate_kernel(
    blocks,
    modules,
    grouped,
    sums,
    out,
    all_sums,
    scaled,
    own,
    far,
    near,
    staged,
    sum_send,
    sum_recv,
    bin_send,
    bin_recv,
    frame_send,
    frame_recv,
    result_send,
    result_recv,
):
    me = lax.axis_index("frame")
    module = lax.axis_index("module")
    bins, per_bin, _ = grouped.shape
    owned = bins // modules
    even = lax.rem(me, 2) == 0
    odd = lax.rem(me, 2) == 1
    has_down = me >= 2
    has_up = me + 2 < blocks
    mate = me + 1 - 2 * lax.rem(me, 2)

    barrier = pltpu.get_barrier_semaphore()

    def greet(frame, mod):
        pl.semaphore_signal(barrier, inc=1, device_id=(frame, mod), device_id_type=MESH)

    for gap in range(1, modules):
        greet(me, lax.rem(module + gap, modules))
    greet(mate, module)

    @pl.when(has_down)
    def _():
        greet(me - 2, module)

    @pl.when(has_up)
    def _():
        greet(me + 2, module)

    peers = modules + has_down.astype(jnp.int32) + has_up.astype(jnp.int32)
    pl.semaphore_wait(barrier, peers)

    def sum_copy(gap):
        return pltpu.make_async_remote_copy(
            src_ref=sums,
            dst_ref=all_sums.at[module],
            send_sem=sum_send.at[gap - 1],
            recv_sem=sum_recv.at[gap - 1],
            device_id=(me, lax.rem(module + gap, modules)),
            device_id_type=MESH,
        )

    for gap in range(1, modules):
        sum_copy(gap).start()
    all_sums[module] = sums[...]
    for gap in range(1, modules):
        sum_copy(gap).wait()
    total = all_sums[0]
    for source in range(1, modules):
        total = total + all_sums[source]
    all_sums[0] = jnp.sqrt(jnp.float32(per_bin * modules)) / total

    def bin_copy(k, gap):
        owner = lax.rem(module + gap, modules)
        return pltpu.make_async_remote_copy(
            src_ref=scaled.at[owner * owned + k],
            dst_ref=own.at[k, pl.ds(pl.multiple_of(module * per_bin, per_bin), per_bin), :],
            send_sem=bin_send.at[k, gap - 1],
            recv_sem=bin_recv.at[k, gap - 1],
            device_id=(me, owner),
            device_id_type=MESH,
        )

    @pl.loop(0, owned)
    def _(k):
        for gap in range(1, modules):
            label = lax.rem(module + gap, modules) * owned + k
            factor = all_sums[0, pl.ds(label, 1), :]
            scaled[label] = (grouped[label] * factor).astype(jnp.bfloat16)
            bin_copy(k, gap).start()
        label = module * owned + k
        factor = all_sums[0, pl.ds(label, 1), :]
        own[k, pl.ds(pl.multiple_of(module * per_bin, per_bin), per_bin), :] = (
            grouped[label] * factor
        ).astype(jnp.bfloat16)

    def frame_copy(k, slot, target, frame):
        return pltpu.make_async_remote_copy(
            src_ref=own.at[k],
            dst_ref=target.at[k],
            send_sem=frame_send.at[slot, k],
            recv_sem=frame_recv.at[slot, k],
            device_id=(frame, module),
            device_id_type=MESH,
        )

    def down_copy(k):
        return frame_copy(k, 0, far, me - 2)

    def up_copy(k):
        return frame_copy(k, 0, far, me + 2)

    def mate_copy(k):
        return frame_copy(k, 1, near, mate)

    def result_copy(k, stage, place, frame):
        return pltpu.make_async_remote_copy(
            src_ref=staged.at[stage, k],
            dst_ref=out.at[k, place],
            send_sem=result_send.at[stage, k],
            recv_sem=result_recv.at[place, k],
            device_id=(frame, module),
            device_id_type=MESH,
        )

    def pass_on(k):
        for gap in range(1, modules):
            bin_copy(k, gap).wait()

        @pl.when(even & has_down)
        def _():
            down_copy(k).start()

        @pl.when(odd)
        def _():
            mate_copy(k).start()

        @pl.when(odd & has_up)
        def _():
            up_copy(k).start()

    def correlate(k):
        out[k, 2] = gram(own[k], own[k])

        @pl.when(even)
        def _():
            mate_copy(k).wait_recv()
            staged[0, k] = gram(near[k], own[k])
            result_copy(k, 0, 1, me + 1).start()
            out[k, 3] = gram(own[k], near[k])

        @pl.when(even & has_up)
        def _():
            up_copy(k).wait_recv()
            staged[1, k] = gram(far[k], own[k])
            result_copy(k, 1, 0, me + 2).start()
            staged[2, k] = gram(far[k], near[k])
            result_copy(k, 2, 1, me + 2).start()
            staged[3, k] = gram(near[k], far[k])
            result_copy(k, 3, 3, me + 1).start()
            out[k, 4] = gram(own[k], far[k])

        @pl.when(odd & has_down)
        def _():
            down_copy(k).wait_recv()
            staged[0, k] = gram(far[k], own[k])
            result_copy(k, 0, 4, me - 2).start()
            out[k, 0] = gram(own[k], far[k])

    @pl.loop(0, owned + 1)
    def _(k):
        @pl.when(k < owned)
        def _():
            pass_on(k)

        @pl.when(k >= 1)
        def _():
            correlate(k - 1)

    @pl.when(me < 2)
    def _():
        out[:, 0] = jnp.zeros_like(out[:, 0])

    @pl.when(me < 1)
    def _():
        out[:, 1] = jnp.zeros_like(out[:, 1])

    @pl.when(me + 1 >= blocks)
    def _():
        out[:, 3] = jnp.zeros_like(out[:, 3])

    @pl.when(me + 2 >= blocks)
    def _():
        out[:, 4] = jnp.zeros_like(out[:, 4])

    @pl.loop(0, owned)
    def _(k):
        @pl.when(even & has_down)
        def _():
            down_copy(k).wait_send()
            result_copy(k, 1, 0, me).wait_recv()
            result_copy(k, 2, 1, me).wait_recv()

        @pl.when(odd)
        def _():
            mate_copy(k).wait_send()
            result_copy(k, 0, 1, me).wait_recv()

        @pl.when(odd & has_up)
        def _():
            up_copy(k).wait_send()
            result_copy(k, 3, 3, me).wait_recv()
            result_copy(k, 0, 4, me).wait_recv()

        @pl.when(even)
        def _():
            result_copy(k, 0, 1, me + 1).wait_send()

        @pl.when(even & has_up)
        def _():
            result_copy(k, 1, 0, me + 2).wait_send()
            result_copy(k, 2, 1, me + 2).wait_send()
            result_copy(k, 3, 3, me + 1).wait_send()

        @pl.when(odd & has_down)
        def _():
            result_copy(k, 0, 4, me - 2).wait_send()


def correlate(grouped, sums):
    bins, per_bin, frames = grouped.shape
    blocks, modules = lax.axis_size("frame"), lax.axis_size("module")
    owned = bins // modules
    pixels = per_bin * modules
    vmem = pl.BlockSpec(memory_space=pltpu.VMEM)
    dma = pltpu.SemaphoreType.DMA
    return pl.pallas_call(
        functools.partial(correlate_kernel, blocks, modules),
        out_shape=jax.ShapeDtypeStruct((owned, 5, frames, frames), jnp.float32),
        in_specs=[vmem, vmem],
        out_specs=vmem,
        scratch_shapes=[
            pltpu.VMEM((modules, bins, frames), jnp.float32),
            pltpu.VMEM((bins, per_bin, frames), jnp.bfloat16),
            pltpu.VMEM((owned, pixels, frames), jnp.bfloat16),
            pltpu.VMEM((owned, pixels, frames), jnp.bfloat16),
            pltpu.VMEM((owned, pixels, frames), jnp.bfloat16),
            pltpu.VMEM((4, owned, frames, frames), jnp.float32),
            dma((modules - 1,)),
            dma((modules - 1,)),
            dma((owned, modules - 1)),
            dma((owned, modules - 1)),
            dma((2, owned)),
            dma((2, owned)),
            dma((4, owned)),
            dma((5, owned)),
        ],
        compiler_params=pltpu.CompilerParams(
            collective_id=0, has_side_effects=True, vmem_limit_bytes=VMEM_BYTES
        ),
    )(grouped, sums)


def per_device(raw_frames, dark_frame, flat_field, membership):
    bins, pixels = membership.shape
    labels = jnp.sum(membership * jnp.arange(bins, dtype=jnp.int32)[:, None], axis=0)
    place = jnp.arange(pixels, dtype=jnp.int32)
    keys = jnp.sort(labels * pixels + place)
    order = keys - place // (pixels // bins) * pixels
    grouped, sums = group_by_bin(order, raw_frames, dark_frame, flat_field, bins)
    return correlate(grouped, sums)[:, None]


def solution(mesh):
    in_specs = (P("frame", "module"), P("module"), P("module"), P(None, "module"))
    out_specs = P("module", "frame", None, None, None)
    return jax.shard_map(
        per_device, mesh=mesh, in_specs=in_specs, out_specs=out_specs, check_vma=False
    )
```

time: 817 us -> 232 us (0.28)
  waiting for transfers between devices: 584 us -> 0 us
  Pallas kernels: 0 us -> 218 us
  local copies, waits for them, and re-layouts: 154 us -> 5.32 us
  other arithmetic: 28.5 us -> 8.54 us
  blocking collectives: 15.4 us -> 0 us
  between operations: 14.2 us -> 0.03 us
  starting transfers between devices: 10.7 us -> 0 us
    unnamed x2 -> x0, waiting for transfers between devices: 423 us -> none
    pallas_call x0 -> x2, Pallas kernels: none -> 218 us  [the longest x1 183 us: correlate(): pl.pallas_call(functools.partial(correlate_kernel, blocks, modules), out_...]
    ppermute x4 -> x0, waiting for transfers between devices: 161 us -> none  [shifted(): lax.ppermute(value, axis, [(source, source + steps) for source in range(l...]
    gather x4 -> x0, local copies, waits for them, and re-layouts: 135 us -> none  [the longest x1 45.5 us: per_device(): dark_sorted = jnp.take(dark_frame, ordering)]
    psum x1 -> x0, blocking collectives: 15.4 us -> none  [per_device(): bin_sums = lax.psum(local_sums, 'module')]
    ppermute x4 -> x0, starting transfers between devices: 10.7 us -> none  [shifted(): lax.ppermute(value, axis, [(source, source + steps) for source in range(l...]
    another operation x1 -> x0, other arithmetic: 9.35 us -> none  [bin_grams(): jnp.stack([jnp.einsum('urp,vrp->ruv', target, partner, preferred_element_...]
    unnamed x13 -> x1, local copies, waits for them, and re-layouts: 13.9 us -> 5.32 us
  transfers between devices with their start and end apart: 5 -> 0, of which waited for: 5 -> 0; matrix products, arithmetic and copies ran while one was open for 1% -> 0% of each run, Pallas kernels for 0% -> 0%
where the time goes in v1:
time: 232 us
  Pallas kernels  218 us (94%)
  other arithmetic  8.54 us (4%)
  local copies, waits for them, and re-layouts  5.32 us (2%)
    pallas_call x1, Pallas kernels, correlate(): pl.pallas_call(functools.partial(correlate_kernel, blocks, modules), out_...  183 us
    pallas_call x1, Pallas kernels, group_by_bin(): pl.pallas_call(functools.partial(group_kernel, per_bin), out_shape=(jax.S...  34.4 us
    sort x1, other arithmetic, per_device(): keys = jnp.sort(labels * pixels + place)  6.77 us
    unnamed x1, local copies, waits for them, and re-layouts  5.32 us

profile of v1, /device:TPU:12, one launch (start us, length us, event | category | flops | bytes accessed | tf_op | source)
XLA Modules:
  0.0 231.7 jit_solution(11391231825345750928)
XLA Ops:
  0.0 1.1 multiply_reduce_fusion
  1.2 6.8 %sort.15 = (s32[8192]{0:T(1024)S(1)}, s32[8192]{0:T(1024)}) sort(s32[8192]{0:T(1024)S(1)} %iota_add_fusion, s32[8192]{0:T(1024)S(1)} %iota.13), dimensions={0}, to_apply=%region_1.0 | sort | flops 106496 | bytes 131072 | tf_op jit(solution)/shard_map/jit(sort)/sort | solution.py:342
  7.9 0.6 fusion.1.order
  8.6 34.4 %shard_map.46 = (f32[16,512,256]{2,1,0:T(8,128)}, f32[16,256]{1,0:T(8,128)}) custom-call(s32[8192]{0:T(1024)} %fusion.1.order, s32[256,8192]{1,0:T(8,128)} %raw.1, f32[1,8192]{1,0:T(1,128)} %bitcast.6, f32[1,8192]{1,0:T(1,128)} %bitcast.7), custom_call_target="tpu_custom_call" | custom-call | tf_op jit(solution)/shard_map/pallas_call | solution.py:46
  42.9 183.4 %shard_map.47 = f32[4,5,256,256]{3,2,1,0:T(8,128)} custom-call(f32[16,512,256]{2,1,0:T(8,128)} %get-tuple-element.10.grouped, f32[16,256]{1,0:T(8,128)} %get-tuple-element.11.sums), custom_call_target="tpu_custom_call" | custom-call | tf_op jit(solution)/shard_map/pallas_call | solution.py:311
  226.4 5.3 %copy.7 = f32[4,1,5,256,256]{4,3,2,1,0:T(8,128)} copy(f32[4,1,5,256,256]{4,3,2,1,0:T(8,128)} %bitcast.5) | data formatting | bytes 10485760
  (2 shorter events, 0.0 us)

commit v2 on v1

--- a/solution.py
+++ b/solution.py
@@ -84,6 +84,7 @@
     own,
     far,
     near,
+    hold,
     staged,
     sum_send,
     sum_recv,
@@ -91,6 +92,8 @@
     bin_recv,
     frame_send,
     frame_recv,
+    relay_send,
+    relay_recv,
     result_send,
     result_recv,
 ):
@@ -103,6 +106,11 @@
     has_down = me >= 2
     has_up = me + 2 < blocks
     mate = me + 1 - 2 * lax.rem(me, 2)
+    relayed = blocks == 8
+    across = lax.rem(me + 4, 8)
+    relaying = (me < 2) | (me >= 6)
+    relay_parity = jnp.where(me >= 6, 1 - lax.rem(me, 2), lax.rem(me, 2))
+    relay_target = jnp.where(even, 2, 5)
 
     barrier = pltpu.get_barrier_semaphore()
 
@@ -112,6 +120,8 @@
     for gap in range(1, modules):
         greet(me, lax.rem(module + gap, modules))
     greet(mate, module)
+    if relayed:
+        greet(across, module)
 
     @pl.when(has_down)
     def _():
@@ -121,7 +131,7 @@
     def _():
         greet(me + 2, module)
 
-    peers = modules + has_down.astype(jnp.int32) + has_up.astype(jnp.int32)
+    peers = modules + int(relayed) + has_down.astype(jnp.int32) + has_up.astype(jnp.int32)
     pl.semaphore_wait(barrier, peers)
 
     def sum_copy(gap):
@@ -168,24 +178,49 @@
             grouped[label] * factor
         ).astype(jnp.bfloat16)
 
-    def frame_copy(k, slot, target, frame):
-        return pltpu.make_async_remote_copy(
-            src_ref=own.at[k],
-            dst_ref=target.at[k],
-            send_sem=frame_send.at[slot, k],
-            recv_sem=frame_recv.at[slot, k],
+    def rows_of(j):
+        source = lax.rem(module + modules - j, modules)
+        return pl.ds(pl.multiple_of(source * per_bin, per_bin), per_bin)
+
+    def frame_copy(k, j, slot, target, frame):
+        return pltpu.make_async_remote_copy(
+            src_ref=own.at[k, rows_of(j), :],
+            dst_ref=target.at[k, rows_of(j), :],
+            send_sem=frame_send.at[slot, k, j],
+            recv_sem=frame_recv.at[slot, k, j],
             device_id=(frame, module),
             device_id_type=MESH,
         )
 
-    def down_copy(k):
-        return frame_copy(k, 0, far, me - 2)
-
-    def up_copy(k):
-        return frame_copy(k, 0, far, me + 2)
-
-    def mate_copy(k):
-        return frame_copy(k, 1, near, mate)
+    def far_copy(k, j):
+        return frame_copy(k, j, 0, far, jnp.where(even, me - 2, me + 2))
+
+    def mate_copy(k, j):
+        return frame_copy(k, j, 1, near, mate)
+
+    def entry_copy(k, j):
+        straight = jnp.where(even, me + 2, me - 2)
+        return pltpu.make_async_remote_copy(
+            src_ref=own.at[k, rows_of(j), :],
+            dst_ref=hold.at[k, rows_of(j), :],
+            send_sem=frame_send.at[0, k, j],
+            recv_sem=relay_recv.at[k, j],
+            device_id=(jnp.where(lax.rem(k, 2) == 0, across, straight), module),
+            device_id_type=MESH,
+        )
+
+    def exit_copy(k, j):
+        return pltpu.make_async_remote_copy(
+            src_ref=hold.at[k, rows_of(j), :],
+            dst_ref=far.at[k, rows_of(j), :],
+            send_sem=relay_send.at[k, j],
+            recv_sem=frame_recv.at[0, k, j],
+            device_id=(relay_target, module),
+            device_id_type=MESH,
+        )
+
+    sends_far = (even & has_down) | (odd & has_up)
+    diagonal = ((me == 3) | (me == 4)) if relayed else None
 
     def result_copy(k, stage, place, frame):
         return pltpu.make_async_remote_copy(
@@ -197,35 +232,48 @@
             device_id_type=MESH,
         )
 
-    def pass_on(k):
-        for gap in range(1, modules):
-            bin_copy(k, gap).wait()
-
-        @pl.when(even & has_down)
-        def _():
-            down_copy(k).start()
-
+    def pass_on(k, j):
         @pl.when(odd)
         def _():
-            mate_copy(k).start()
-
-        @pl.when(odd & has_up)
-        def _():
-            up_copy(k).start()
+            mate_copy(k, j).start()
+
+        if relayed:
+            @pl.when(diagonal)
+            def _():
+                entry_copy(k, j).start()
+
+            @pl.when(sends_far & jnp.logical_not(diagonal))
+            def _():
+                far_copy(k, j).start()
+        else:
+            @pl.when(sends_far)
+            def _():
+                far_copy(k, j).start()
+
+    def relay(k, j):
+        if relayed:
+            @pl.when(relaying & (lax.rem(k, 2) == relay_parity))
+            def _():
+                entry_copy(k, j).wait_recv()
+                exit_copy(k, j).start()
+
+    def await_frames(k, copy):
+        for j in range(modules):
+            copy(k, j).wait_recv()
 
     def correlate(k):
         out[k, 2] = gram(own[k], own[k])
 
         @pl.when(even)
         def _():
-            mate_copy(k).wait_recv()
+            await_frames(k, mate_copy)
             staged[0, k] = gram(near[k], own[k])
             result_copy(k, 0, 1, me + 1).start()
             out[k, 3] = gram(own[k], near[k])
 
         @pl.when(even & has_up)
         def _():
-            up_copy(k).wait_recv()
+            await_frames(k, far_copy)
             staged[1, k] = gram(far[k], own[k])
             result_copy(k, 1, 0, me + 2).start()
             staged[2, k] = gram(far[k], near[k])
@@ -236,18 +284,33 @@
 
         @pl.when(odd & has_down)
         def _():
-            down_copy(k).wait_recv()
+            await_frames(k, far_copy)
             staged[0, k] = gram(far[k], own[k])
             result_copy(k, 0, 4, me - 2).start()
             out[k, 0] = gram(own[k], far[k])
 
-    @pl.loop(0, owned + 1)
-    def _(k):
+    for k in range(owned):
+        pass_on(k, 0)
+    for k in range(owned):
+        relay(k, 0)
+    gaps = modules - 1
+
+    @pl.loop(0, (owned + 1) * gaps)
+    def _(step):
+        k, j = step // gaps, lax.rem(step, gaps) + 1
+
         @pl.when(k < owned)
         def _():
-            pass_on(k)
-
-        @pl.when(k >= 1)
+            bin_copy(k, j).wait()
+            pass_on(k, j)
+
+        earlier = step - 1
+
+        @pl.when((earlier >= 0) & (earlier < owned * gaps))
+        def _():
+            relay(earlier // gaps, lax.rem(earlier, gaps) + 1)
+
+        @pl.when((k >= 1) & (j == gaps))
         def _():
             correlate(k - 1)
 
@@ -271,20 +334,30 @@
     def _(k):
         @pl.when(even & has_down)
         def _():
-            down_copy(k).wait_send()
             result_copy(k, 1, 0, me).wait_recv()
             result_copy(k, 2, 1, me).wait_recv()
 
         @pl.when(odd)
         def _():
-            mate_copy(k).wait_send()
+            for j in range(modules):
+                mate_copy(k, j).wait_send()
             result_copy(k, 0, 1, me).wait_recv()
 
+        @pl.when(sends_far)
+        def _():
+            for j in range(modules):
+                far_copy(k, j).wait_send()
+
         @pl.when(odd & has_up)
         def _():
-            up_copy(k).wait_send()
             result_copy(k, 3, 3, me).wait_recv()
             result_copy(k, 0, 4, me).wait_recv()
+
+        if relayed:
+            @pl.when(relaying & (lax.rem(k, 2) == relay_parity))
+            def _():
+                for j in range(modules):
+                    exit_copy(k, j).wait_send()
 
         @pl.when(even)
         def _():
@@ -319,13 +392,16 @@
             pltpu.VMEM((owned, pixels, frames), jnp.bfloat16),
             pltpu.VMEM((owned, pixels, frames), jnp.bfloat16),
             pltpu.VMEM((owned, pixels, frames), jnp.bfloat16),
+            pltpu.VMEM((owned, pixels, frames), jnp.bfloat16),
             pltpu.VMEM((4, owned, frames, frames), jnp.float32),
             dma((modules - 1,)),
             dma((modules - 1,)),
             dma((owned, modules - 1)),
             dma((owned, modules - 1)),
-            dma((2, owned)),
-            dma((2, owned)),
+            dma((2, owned, modules)),
+            dma((2, owned, modules)),
+            dma((owned, modules)),
+            dma((owned, modules)),
             dma((4, owned)),
             dma((5, owned)),
         ],

time: 232 us -> 201 us (0.87)
  Pallas kernels: 218 us -> 187 us
    pallas_call x1, Pallas kernels: 183 us -> 152 us  [correlate(): pl.pallas_call(functools.partial(correlate_kernel, blocks, modules), out_...]
where the time goes in v2:
time: 201 us
  Pallas kernels  187 us (93%)
  other arithmetic  8.54 us (4%)
  local copies, waits for them, and re-layouts  5.32 us (3%)
    pallas_call x1, Pallas kernels, correlate(): pl.pallas_call(functools.partial(correlate_kernel, blocks, modules), out_...  152 us
    pallas_call x1, Pallas kernels, group_by_bin(): pl.pallas_call(functools.partial(group_kernel, per_bin), out_shape=(jax.S...  34.4 us
    sort x1, other arithmetic, per_device(): keys = jnp.sort(labels * pixels + place)  6.77 us
    unnamed x1, local copies, waits for them, and re-layouts  5.32 us

profile of v2, /device:TPU:12, one launch (start us, length us, event | category | flops | bytes accessed | tf_op | source)
XLA Modules:
  0.0 200.7 jit_solution(13432715341768307425)
XLA Ops:
  0.0 1.1 multiply_reduce_fusion
  1.2 6.8 %sort.15 = (s32[8192]{0:T(1024)S(1)}, s32[8192]{0:T(1024)}) sort(s32[8192]{0:T(1024)S(1)} %iota_add_fusion, s32[8192]{0:T(1024)S(1)} %iota.13), dimensions={0}, to_apply=%region_1.0 | sort | flops 106496 | bytes 131072 | tf_op jit(solution)/shard_map/jit(sort)/sort | solution.py:418
  7.9 0.6 fusion.1.order
  8.6 34.4 %shard_map.46 = (f32[16,512,256]{2,1,0:T(8,128)}, f32[16,256]{1,0:T(8,128)}) custom-call(s32[8192]{0:T(1024)} %fusion.1.order, s32[256,8192]{1,0:T(8,128)} %raw.1, f32[1,8192]{1,0:T(1,128)} %bitcast.6, f32[1,8192]{1,0:T(1,128)} %bitcast.7), custom_call_target="tpu_custom_call" | custom-call | tf_op jit(solution)/shard_map/pallas_call | solution.py:46
  42.9 152.4 %shard_map.47 = f32[4,5,256,256]{3,2,1,0:T(8,128)} custom-call(f32[16,512,256]{2,1,0:T(8,128)} %get-tuple-element.10.grouped, f32[16,256]{1,0:T(8,128)} %get-tuple-element.11.sums), custom_call_target="tpu_custom_call" | custom-call | tf_op jit(solution)/shard_map/pallas_call | solution.py:384
  195.4 5.3 %copy.7 = f32[4,1,5,256,256]{4,3,2,1,0:T(8,128)} copy(f32[4,1,5,256,256]{4,3,2,1,0:T(8,128)} %bitcast.5) | data formatting | bytes 10485760
  (2 shorter events, 0.0 us)

commit v3 on v2

--- a/solution.py
+++ b/solution.py
@@ -11,60 +11,44 @@
 VMEM_BYTES = 60 * 1024 * 1024
 
 
-def group_kernel(per_bin, order, raw, dark, flat, grouped, sums, turned):
-    step = pl.program_id(0)
-    chunk = raw.shape[1]
+def turn_kernel(raw, dark, flat, members, turned, sums):
+    @pl.when(pl.program_id(0) == 0)
+    def _():
+        sums[...] = jnp.zeros_like(sums)
+
     intensity = (raw[...].astype(jnp.float32) - dark[...]) * flat[...]
-    turned[pl.ds(pl.multiple_of(step * chunk, chunk), chunk), :] = intensity.T
-
-    @pl.when(step == pl.num_programs(0) - 1)
-    def _():
-        frames = turned.shape[1]
-        lane = lax.broadcasted_iota(jnp.int32, (8, frames), 0)
-
-        @pl.loop(0, grouped.shape[0])
-        def _(label):
-            base = label * per_bin
-
-            def rows(group, total):
-                first = pl.multiple_of(group * 8, 8)
-                tile = jnp.broadcast_to(turned[pl.ds(order[base + first], 1), :], (8, frames))
-                for row in range(1, 8):
-                    line = turned[pl.ds(order[base + first + row], 1), :]
-                    tile = jnp.where(lane == row, line, tile)
-                grouped[label, pl.ds(first, 8), :] = tile
-                return total + tile
-
-            total = lax.fori_loop(0, per_bin // 8, rows, jnp.zeros((8, frames), jnp.float32), unroll=4)
-            sums[pl.ds(label, 1), :] = jnp.sum(total, axis=0, keepdims=True)
-
-
-def group_by_bin(order, raw_frames, dark_frame, flat_field, bins):
+    lines = intensity.T
+    turned[...] = lines
+    sums[...] += jnp.dot(
+        members[...].astype(jnp.float32),
+        lines,
+        precision=lax.Precision.HIGHEST,
+        preferred_element_type=jnp.float32,
+    )
+
+
+def turn(raw_frames, dark_frame, flat_field, membership):
     frames, pixels = raw_frames.shape
-    per_bin = pixels // bins
-    chunk = per_bin
+    bins = membership.shape[0]
+    chunk = pixels // bins
     return pl.pallas_call(
-        functools.partial(group_kernel, per_bin),
+        turn_kernel,
         out_shape=(
-            jax.ShapeDtypeStruct((bins, per_bin, frames), jnp.float32),
+            jax.ShapeDtypeStruct((pixels, frames), jnp.float32),
             jax.ShapeDtypeStruct((bins, frames), jnp.float32),
         ),
-        grid_spec=pltpu.PrefetchScalarGridSpec(
-            num_scalar_prefetch=1,
-            grid=(pixels // chunk,),
-            in_specs=[
-                pl.BlockSpec((frames, chunk), lambda i, o: (0, i)),
-                pl.BlockSpec((1, chunk), lambda i, o: (0, i)),
-                pl.BlockSpec((1, chunk), lambda i, o: (0, i)),
-            ],
-            out_specs=(
-                pl.BlockSpec((bins, per_bin, frames), lambda i, o: (0, 0, 0)),
-                pl.BlockSpec((bins, frames), lambda i, o: (0, 0)),
-            ),
-            scratch_shapes=[pltpu.VMEM((pixels, frames), jnp.float32)],
+        grid=(pixels // chunk,),
+        in_specs=[
+            pl.BlockSpec((frames, chunk), lambda i: (0, i)),
+            pl.BlockSpec((1, chunk), lambda i: (0, i)),
+            pl.BlockSpec((1, chunk), lambda i: (0, i)),
+            pl.BlockSpec((bins, chunk), lambda i: (0, i)),
+        ],
+        out_specs=(
+            pl.BlockSpec((chunk, frames), lambda i: (i, 0)),
+            pl.BlockSpec((bins, frames), lambda i: (0, 0)),
         ),
-        compiler_params=pltpu.CompilerParams(vmem_limit_bytes=VMEM_BYTES),
-    )(order, raw_frames, dark_frame[None, :], flat_field[None, :])
+    )(raw_frames, dark_frame[None, :], flat_field[None, :], membership)
 
 
 def gram(left, right):
@@ -76,7 +60,8 @@
 def correlate_kernel(
     blocks,
     modules,
-    grouped,
+    order,
+    turned,
     sums,
     out,
     all_sums,
@@ -99,7 +84,9 @@
 ):
     me = lax.axis_index("frame")
     module = lax.axis_index("module")
-    bins, per_bin, _ = grouped.shape
+    pixels, frames = turned.shape
+    bins = sums.shape[0]
+    per_bin = pixels // bins
     owned = bins // modules
     even = lax.rem(me, 2) == 0
     odd = lax.rem(me, 2) == 1
@@ -165,18 +152,26 @@
             device_id_type=MESH,
         )
 
-    @pl.loop(0, owned)
-    def _(k):
-        for gap in range(1, modules):
-            label = lax.rem(module + gap, modules) * owned + k
-            factor = all_sums[0, pl.ds(label, 1), :]
-            scaled[label] = (grouped[label] * factor).astype(jnp.bfloat16)
-            bin_copy(k, gap).start()
-        label = module * owned + k
+    row_index = lax.broadcasted_iota(jnp.int32, (8, frames), 0)
+
+    def fill(label, target, first):
         factor = all_sums[0, pl.ds(label, 1), :]
-        own[k, pl.ds(pl.multiple_of(module * per_bin, per_bin), per_bin), :] = (
-            grouped[label] * factor
-        ).astype(jnp.bfloat16)
+
+        def tile(start):
+            lines = jnp.broadcast_to(turned[pl.ds(order[start], 1), :], (8, frames))
+            for row in range(1, 8):
+                line = turned[pl.ds(order[start + row], 1), :]
+                lines = jnp.where(row_index == row, line, lines)
+            return lines * factor
+
+        def tiles(group, carry):
+            start = label * per_bin + group * 16
+            both = jnp.concatenate([tile(start), tile(start + 8)], axis=0)
+            rows = pl.ds(pl.multiple_of(first + group * 16, 16), 16)
+            target[rows, :] = both.astype(jnp.bfloat16)
+            return carry
+
+        lax.fori_loop(0, per_bin // 16, tiles, 0, unroll=4)
 
     def rows_of(j):
         source = lax.rem(module + modules - j, modules)
@@ -289,8 +284,17 @@
             result_copy(k, 0, 4, me - 2).start()
             out[k, 0] = gram(own[k], far[k])
 
-    for k in range(owned):
+    @pl.loop(0, owned)
+    def _(k):
+        @pl.loop(1, modules)
+        def _(gap):
+            label = lax.rem(module + gap, modules) * owned + k
+            fill(label, scaled.at[label], 0)
+            bin_copy(k, gap).start()
+
+        fill(module * owned + k, own.at[k], module * per_bin)
         pass_on(k, 0)
+
     for k in range(owned):
         relay(k, 0)
     gaps = modules - 1
@@ -374,25 +378,26 @@
             result_copy(k, 0, 4, me - 2).wait_send()
 
 
-def correlate(grouped, sums):
-    bins, per_bin, frames = grouped.shape
+def correlate(order, turned, sums):
+    (pixels, frames), bins = turned.shape, sums.shape[0]
+    per_bin = pixels // bins
     blocks, modules = lax.axis_size("frame"), lax.axis_size("module")
     owned = bins // modules
-    pixels = per_bin * modules
+    gathered = per_bin * modules
     vmem = pl.BlockSpec(memory_space=pltpu.VMEM)
     dma = pltpu.SemaphoreType.DMA
     return pl.pallas_call(
         functools.partial(correlate_kernel, blocks, modules),
         out_shape=jax.ShapeDtypeStruct((owned, 5, frames, frames), jnp.float32),
-        in_specs=[vmem, vmem],
+        in_specs=[pl.BlockSpec(memory_space=pltpu.SMEM), vmem, vmem],
         out_specs=vmem,
         scratch_shapes=[
             pltpu.VMEM((modules, bins, frames), jnp.float32),
             pltpu.VMEM((bins, per_bin, frames), jnp.bfloat16),
-            pltpu.VMEM((owned, pixels, frames), jnp.bfloat16),
-            pltpu.VMEM((owned, pixels, frames), jnp.bfloat16),
-            pltpu.VMEM((owned, pixels, frames), jnp.bfloat16),
-            pltpu.VMEM((owned, pixels, frames), jnp.bfloat16),
+            pltpu.VMEM((owned, gathered, frames), jnp.bfloat16),
+            pltpu.VMEM((owned, gathered, frames), jnp.bfloat16),
+            pltpu.VMEM((owned, gathered, frames), jnp.bfloat16),
+            pltpu.VMEM((owned, gathered, frames), jnp.bfloat16),
             pltpu.VMEM((4, owned, frames, frames), jnp.float32),
             dma((modules - 1,)),
             dma((modules - 1,)),
@@ -408,7 +413,7 @@
         compiler_params=pltpu.CompilerParams(
             collective_id=0, has_side_effects=True, vmem_limit_bytes=VMEM_BYTES
         ),
-    )(grouped, sums)
+    )(order, turned, sums)
 
 
 def per_device(raw_frames, dark_frame, flat_field, membership):
@@ -417,8 +422,8 @@
     place = jnp.arange(pixels, dtype=jnp.int32)
     keys = jnp.sort(labels * pixels + place)
     order = keys - place // (pixels // bins) * pixels
-    grouped, sums = group_by_bin(order, raw_frames, dark_frame, flat_field, bins)
-    return correlate(grouped, sums)[:, None]
+    turned, sums = turn(raw_frames, dark_frame, flat_field, membership)
+    return correlate(order, turned, sums)[:, None]
 
 
 def solution(mesh):

time: 201 us -> 182 us (0.905)
  Pallas kernels: 187 us -> 167 us
    pallas_call x1, Pallas kernels: 34.4 us -> 13.9 us  [turn(): pl.pallas_call(turn_kernel, out_shape=(jax.ShapeDtypeStruct((pixels, fram...]
where the time goes in v3:
time: 182 us; the launch traced here: 181 us
  Pallas kernels  167 us (92%)
  other arithmetic  8.54 us (5%)
  local copies, waits for them, and re-layouts  5.32 us (3%)
    pallas_call x1, Pallas kernels, correlate(): pl.pallas_call(functools.partial(correlate_kernel, blocks, modules), out_...  153 us
    pallas_call x1, Pallas kernels, turn(): pl.pallas_call(turn_kernel, out_shape=(jax.ShapeDtypeStruct((pixels, fram...  13.9 us
    sort x1, other arithmetic, per_device(): keys = jnp.sort(labels * pixels + place)  6.77 us
    unnamed x1, local copies, waits for them, and re-layouts  5.32 us

profile of v3, /device:TPU:12, one launch (start us, length us, event | category | flops | bytes accessed | tf_op | source)
XLA Modules:
  0.0 181.1 jit_solution(9069616469295644274)
XLA Ops:
  0.0 1.1 multiply_reduce_fusion
  1.2 6.8 %sort.15 = (s32[8192]{0:T(1024)S(1)}, s32[8192]{0:T(1024)}) sort(s32[8192]{0:T(1024)S(1)} %iota_add_fusion, s32[8192]{0:T(1024)S(1)} %iota.13), dimensions={0}, to_apply=%region_1.0 | sort | flops 106496 | bytes 131072 | tf_op jit(solution)/shard_map/jit(sort)/sort | solution.py:423
  7.9 0.6 fusion.1.order
  8.6 13.9 %shard_map.46 = (f32[8192,256]{1,0:T(8,128)}, f32[16,256]{1,0:T(8,128)}) custom-call(s32[256,8192]{1,0:T(8,128)} %raw.1, f32[1,8192]{1,0:T(1,128)} %bitcast.6, f32[1,8192]{1,0:T(1,128)} %bitcast.7, s32[16,8192]{1,0:T(8,128)} %members.1), custom_call_target="tpu_custom_call" | custom-call | tf_op jit(solution)/shard_map/pallas_call | solution.py:34
  22.5 153.3 %shard_map.47 = f32[4,5,256,256]{3,2,1,0:T(8,128)} custom-call(s32[8192]{0:T(1024)} %fusion.1.order, f32[8192,256]{1,0:T(8,128)} %get-tuple-element.10.turned, f32[16,256]{1,0:T(8,128)} %get-tuple-element.11.sums), custom_call_target="tpu_custom_call" | custom-call | tf_op jit(solution)/shard_map/pallas_call | solution.py:389
  175.8 5.3 %copy.7 = f32[4,1,5,256,256]{4,3,2,1,0:T(8,128)} copy(f32[4,1,5,256,256]{4,3,2,1,0:T(8,128)} %bitcast.5) | data formatting | bytes 10485760
  (2 shorter events, 0.0 us)

commit v4 on v3

--- a/solution.py
+++ b/solution.py
@@ -141,13 +141,19 @@
         total = total + all_sums[source]
     all_sums[0] = jnp.sqrt(jnp.float32(per_bin * modules)) / total
 
-    def bin_copy(k, gap):
+    half = per_bin // 2
+    parts = 2 * modules
+
+    def bin_copy(k, piece):
+        gap, part = piece // 2, lax.rem(piece, 2)
         owner = lax.rem(module + gap, modules)
-        return pltpu.make_async_remote_copy(
-            src_ref=scaled.at[owner * owned + k],
-            dst_ref=own.at[k, pl.ds(pl.multiple_of(module * per_bin, per_bin), per_bin), :],
-            send_sem=bin_send.at[k, gap - 1],
-            recv_sem=bin_recv.at[k, gap - 1],
+        start = pl.multiple_of(part * half, half)
+        landing = pl.multiple_of(module * per_bin + part * half, half)
+        return pltpu.make_async_remote_copy(
+            src_ref=scaled.at[owner * owned + k, pl.ds(start, half), :],
+            dst_ref=own.at[k, pl.ds(landing, half), :],
+            send_sem=bin_send.at[k, piece],
+            recv_sem=bin_recv.at[k, piece],
             device_id=(me, owner),
             device_id_type=MESH,
         )
@@ -174,8 +180,8 @@
         lax.fori_loop(0, per_bin // 16, tiles, 0, unroll=4)
 
     def rows_of(j):
-        source = lax.rem(module + modules - j, modules)
-        return pl.ds(pl.multiple_of(source * per_bin, per_bin), per_bin)
+        source = lax.rem(module + modules - j // 2, modules)
+        return pl.ds(pl.multiple_of(source * per_bin + lax.rem(j, 2) * half, half), half)
 
     def frame_copy(k, j, slot, target, frame):
         return pltpu.make_async_remote_copy(
@@ -253,7 +259,7 @@
                 exit_copy(k, j).start()
 
     def await_frames(k, copy):
-        for j in range(modules):
+        for j in range(parts):
             copy(k, j).wait_recv()
 
     def correlate(k):
@@ -290,33 +296,43 @@
         def _(gap):
             label = lax.rem(module + gap, modules) * owned + k
             fill(label, scaled.at[label], 0)
-            bin_copy(k, gap).start()
+            bin_copy(k, 2 * gap).start()
+            bin_copy(k, 2 * gap + 1).start()
 
         fill(module * owned + k, own.at[k], module * per_bin)
         pass_on(k, 0)
-
-    for k in range(owned):
+        pass_on(k, 1)
+
+    @pl.loop(0, owned)
+    def _(k):
         relay(k, 0)
-    gaps = modules - 1
-
-    @pl.loop(0, (owned + 1) * gaps)
-    def _(step):
-        k, j = step // gaps, lax.rem(step, gaps) + 1
-
-        @pl.when(k < owned)
-        def _():
-            bin_copy(k, j).wait()
-            pass_on(k, j)
-
-        earlier = step - 1
-
-        @pl.when((earlier >= 0) & (earlier < owned * gaps))
-        def _():
-            relay(earlier // gaps, lax.rem(earlier, gaps) + 1)
-
-        @pl.when((k >= 1) & (j == gaps))
-        def _():
-            correlate(k - 1)
+        relay(k, 1)
+
+    light = jnp.where(lax.rem(module, 2) == 1, 1, modules - 1)
+    heavy = [lax.rem(light + i - 1, modules - 1) + 1 for i in range(1, modules - 1)]
+
+    def receive(k, gaps):
+        pieces = [2 * gap + part for part in range(2) for gap in gaps]
+        for index, piece in enumerate(pieces):
+            bin_copy(k, piece).wait()
+            pass_on(k, piece)
+            if index:
+                relay(k, pieces[index - 1])
+        relay(k, pieces[-1])
+
+    @pl.loop(0, owned + 2)
+    def _(turn_index):
+        @pl.when(turn_index < owned)
+        def _():
+            receive(turn_index, [light])
+
+        @pl.when((turn_index >= 1) & (turn_index <= owned))
+        def _():
+            receive(turn_index - 1, heavy)
+
+        @pl.when(turn_index >= 2)
+        def _():
+            correlate(turn_index - 2)
 
     @pl.when(me < 2)
     def _():
@@ -343,13 +359,13 @@
 
         @pl.when(odd)
         def _():
-            for j in range(modules):
+            for j in range(parts):
                 mate_copy(k, j).wait_send()
             result_copy(k, 0, 1, me).wait_recv()
 
         @pl.when(sends_far)
         def _():
-            for j in range(modules):
+            for j in range(parts):
                 far_copy(k, j).wait_send()
 
         @pl.when(odd & has_up)
@@ -360,7 +376,7 @@
         if relayed:
             @pl.when(relaying & (lax.rem(k, 2) == relay_parity))
             def _():
-                for j in range(modules):
+                for j in range(parts):
                     exit_copy(k, j).wait_send()
 
         @pl.when(even)
@@ -401,12 +417,12 @@
             pltpu.VMEM((4, owned, frames, frames), jnp.float32),
             dma((modules - 1,)),
             dma((modules - 1,)),
-            dma((owned, modules - 1)),
-            dma((owned, modules - 1)),
-            dma((2, owned, modules)),
-            dma((2, owned, modules)),
-            dma((owned, modules)),
-            dma((owned, modules)),
+            dma((owned, 2 * modules)),
+            dma((owned, 2 * modules)),
+            dma((2, owned, 2 * modules)),
+            dma((2, owned, 2 * modules)),
+            dma((owned, 2 * modules)),
+            dma((owned, 2 * modules)),
             dma((4, owned)),
             dma((5, owned)),
         ],

time: 182 us -> 194 us (1.066)
  the two profiles are of different devices: /device:TPU:12 before, /device:TPU:20 now
where the time goes in v4:
time: 194 us; the launch traced here: 193 us
  Pallas kernels  179 us (92%)
  other arithmetic  8.54 us (4%)
  local copies, waits for them, and re-layouts  5.32 us (3%)
    pallas_call x1, Pallas kernels, correlate(): pl.pallas_call(functools.partial(correlate_kernel, blocks, modules), out_...  165 us
    pallas_call x1, Pallas kernels, turn(): pl.pallas_call(turn_kernel, out_shape=(jax.ShapeDtypeStruct((pixels, fram...  13.9 us
    sort x1, other arithmetic, per_device(): keys = jnp.sort(labels * pixels + place)  6.77 us
    unnamed x1, local copies, waits for them, and re-layouts  5.32 us

profile of v4, /device:TPU:20, one launch (start us, length us, event | category | flops | bytes accessed | tf_op | source)
XLA Modules:
  0.0 193.3 jit_solution(17051016264313365333)
XLA Ops:
  0.0 1.1 multiply_reduce_fusion
  1.2 6.8 %sort.15 = (s32[8192]{0:T(1024)S(1)}, s32[8192]{0:T(1024)}) sort(s32[8192]{0:T(1024)S(1)} %iota_add_fusion, s32[8192]{0:T(1024)S(1)} %iota.13), dimensions={0}, to_apply=%region_1.0 | sort | flops 106496 | bytes 131072 | tf_op jit(solution)/shard_map/jit(sort)/sort | solution.py:439
  7.9 0.6 fusion.1.order
  8.6 13.9 %shard_map.46 = (f32[8192,256]{1,0:T(8,128)}, f32[16,256]{1,0:T(8,128)}) custom-call(s32[256,8192]{1,0:T(8,128)} %raw.1, f32[1,8192]{1,0:T(1,128)} %bitcast.6, f32[1,8192]{1,0:T(1,128)} %bitcast.7, s32[16,8192]{1,0:T(8,128)} %members.1), custom_call_target="tpu_custom_call" | custom-call | tf_op jit(solution)/shard_map/pallas_call | solution.py:34
  22.5 165.5 %shard_map.47 = f32[4,5,256,256]{3,2,1,0:T(8,128)} custom-call(s32[8192]{0:T(1024)} %fusion.1.order, f32[8192,256]{1,0:T(8,128)} %get-tuple-element.10.turned, f32[16,256]{1,0:T(8,128)} %get-tuple-element.11.sums), custom_call_target="tpu_custom_call" | custom-call | tf_op jit(solution)/shard_map/pallas_call | solution.py:405
  187.9 5.3 %copy.7 = f32[4,1,5,256,256]{4,3,2,1,0:T(8,128)} copy(f32[4,1,5,256,256]{4,3,2,1,0:T(8,128)} %bitcast.5) | data formatting | bytes 10485760
  (2 shorter events, 0.0 us)

commit v5 on v4

--- a/solution.py
+++ b/solution.py
@@ -308,11 +308,8 @@
         relay(k, 0)
         relay(k, 1)
 
-    light = jnp.where(lax.rem(module, 2) == 1, 1, modules - 1)
-    heavy = [lax.rem(light + i - 1, modules - 1) + 1 for i in range(1, modules - 1)]
-
     def receive(k, gaps):
-        pieces = [2 * gap + part for part in range(2) for gap in gaps]
+        pieces = [2 * gap + part for gap in gaps for part in range(2)]
         for index, piece in enumerate(pieces):
             bin_copy(k, piece).wait()
             pass_on(k, piece)
@@ -320,19 +317,15 @@
                 relay(k, pieces[index - 1])
         relay(k, pieces[-1])
 
-    @pl.loop(0, owned + 2)
+    @pl.loop(0, owned + 1)
     def _(turn_index):
         @pl.when(turn_index < owned)
         def _():
-            receive(turn_index, [light])
-
-        @pl.when((turn_index >= 1) & (turn_index <= owned))
-        def _():
-            receive(turn_index - 1, heavy)
-
-        @pl.when(turn_index >= 2)
-        def _():
-            correlate(turn_index - 2)
+            receive(turn_index, range(1, modules))
+
+        @pl.when(turn_index >= 1)
+        def _():
+            correlate(turn_index - 1)
 
     @pl.when(me < 2)
     def _():

time: 194 us -> 180 us (0.928)
  the two profiles are of different devices: /device:TPU:20 before, /device:TPU:12 now
where the time goes in v5:
time: 180 us
  Pallas kernels  166 us (92%)
  other arithmetic  8.54 us (5%)
  local copies, waits for them, and re-layouts  5.32 us (3%)
    pallas_call x1, Pallas kernels, correlate(): pl.pallas_call(functools.partial(correlate_kernel, blocks, modules), out_...  152 us
    pallas_call x1, Pallas kernels, turn(): pl.pallas_call(turn_kernel, out_shape=(jax.ShapeDtypeStruct((pixels, fram...  13.9 us
    sort x1, other arithmetic, per_device(): keys = jnp.sort(labels * pixels + place)  6.77 us
    unnamed x1, local copies, waits for them, and re-layouts  5.32 us

profile of v5, /device:TPU:12, one launch (start us, length us, event | category | flops | bytes accessed | tf_op | source)
XLA Modules:
  0.0 179.6 jit_solution(9637067017618790883)
XLA Ops:
  0.0 1.1 multiply_reduce_fusion
  1.2 6.8 %sort.15 = (s32[8192]{0:T(1024)S(1)}, s32[8192]{0:T(1024)}) sort(s32[8192]{0:T(1024)S(1)} %iota_add_fusion, s32[8192]{0:T(1024)S(1)} %iota.13), dimensions={0}, to_apply=%region_1.0 | sort | flops 106496 | bytes 131072 | tf_op jit(solution)/shard_map/jit(sort)/sort | solution.py:432
  7.9 0.6 fusion.1.order
  8.6 13.9 %shard_map.46 = (f32[8192,256]{1,0:T(8,128)}, f32[16,256]{1,0:T(8,128)}) custom-call(s32[256,8192]{1,0:T(8,128)} %raw.1, f32[1,8192]{1,0:T(1,128)} %bitcast.6, f32[1,8192]{1,0:T(1,128)} %bitcast.7, s32[16,8192]{1,0:T(8,128)} %members.1), custom_call_target="tpu_custom_call" | custom-call | tf_op jit(solution)/shard_map/pallas_call | solution.py:34
  22.5 151.8 %shard_map.47 = f32[4,5,256,256]{3,2,1,0:T(8,128)} custom-call(s32[8192]{0:T(1024)} %fusion.1.order, f32[8192,256]{1,0:T(8,128)} %get-tuple-element.10.turned, f32[16,256]{1,0:T(8,128)} %get-tuple-element.11.sums), custom_call_target="tpu_custom_call" | custom-call | tf_op jit(solution)/shard_map/pallas_call | solution.py:398
  174.2 5.3 %copy.7 = f32[4,1,5,256,256]{4,3,2,1,0:T(8,128)} copy(f32[4,1,5,256,256]{4,3,2,1,0:T(8,128)} %bitcast.5) | data formatting | bytes 10485760
  (2 shorter events, 0.0 us)
